TPU v7x, 128 devices: a whole 4x4x4 slice. The times are simulated.
128 devices in a mesh: grp: 4 (over y), slab: 32 (over z, x, core).
Axes of the slice: x: 4, y: 4, z: 4, core: 2. Of those that a mesh axis runs over, the one named last changes fastest.
Arguments:
- charges: float32 [524288], P(('grp', 'slab')), may hold values from -6 to 6
- projection: float32 [16384, 64, 64], P(('grp', 'slab')), may hold values from -0.75 to 0.75
- stencil_block: int32 [16384], P(('grp', 'slab')), may hold values from 0 to 63
- stencil_dest: int32 [16384, 1], P(('grp', 'slab')), may hold values from 0 to 127; in each aligned block of 128 rows (0 to 127, 128 to 255, ...) at most 2 rows name the same one
- stencil_cells: int32 [32768, 64], P(('grp', 'slab')), may hold values from 0 to 131071
- green_spectrum: float32 [512, 512, 512], P(('grp', 'slab')), may hold values from 2 to 330, as said below
- near_blocks: float32 [32768, 64, 64], P(('grp', 'slab')), may hold values from -0.375 to 0.375
- near_target: int32 [32768], P(('grp', 'slab')), may hold values from 0 to 63
- near_source: int32 [32768], P(('grp', 'slab')), may hold values from 0 to 191
Outputs:
- potential: float32 [524288], P(('grp', 'slab'))
Inputs may be any that keep to these rules, and one draw needn't show every extreme that they name: `stencil_dest`: among the rows of one device (aligned blocks of 128 rows) at most 2 name the same device, and in some such block one device is named exactly 2 times. `green_spectrum`: Positive, and unchanged when any one frequency index f of a dimension of length L is replaced by (L - f) mod L.
All inputs are finite; a program needn't handle non-finite values.
Results may differ from a plain program's by a relative error of at most 0.00005.
Values sent between devices are 32-bit elements; how exact they have to be, the bound alone decides.
A program may use at most 64 MiB of HBM per device.

v0:
```python
import functools
import math

import jax
import jax.numpy as jnp
import numpy as np
from jax import lax
from jax.experimental import pallas as pl
from jax.experimental.pallas import tpu as pltpu
from jax.sharding import PartitionSpec as P

GX = 256
GY = 256
GZ = 256
BLK = 64
STEN = 64
LANES = 128


highest = lax.Precision.HIGHEST
NN = (((1,), (0,)), ((), ()))
NT = (((1,), (1,)), ((), ()))


def with_halo(x, sides, width):
    for axis, dim in sides:
        devices, length = (lax.axis_size(axis), x.shape[dim])
        up = [(i, (i + 1) % devices) for i in range(devices - 1)]
        down = [(j, i) for i, j in up]
        last = lax.slice_in_dim(x, length - width, length, axis=dim)
        first = lax.slice_in_dim(x, 0, width, axis=dim)
        before = lax.ppermute(last, axis, up)
        after = lax.ppermute(first, axis, down)
        x = jnp.concatenate([before, x, after], axis=dim)
    return x


def one_hot_rows(indices, count):
    return (indices[:, None] == jnp.arange(count, dtype=jnp.int32)[None, :]).astype(jnp.float32)


def cas_table(rows, columns, length):
    phase = np.outer(np.arange(rows), np.arange(columns)) % length * (2.0 * math.pi / length)
    return (np.cos(phase) + np.sin(phase)).astype(np.float32)


def lane_parts(table):
    return np.stack(np.split(table, table.shape[1] // LANES, axis=1))


def halves(x):
    top = x.astype(jnp.bfloat16)
    return top, (x - top.astype(jnp.float32)).astype(jnp.bfloat16)


def product(left, right, form):
    def one(a, b):
        return lax.dot_general(a, b, form, preferred_element_type=jnp.float32)

    return one(left[0], right[0]) + one(left[0], right[1]) + one(left[1], right[0])


def whole_kernel(
    devices, slab, values, cells, table, table_t, green_hbm, out,
    rows_hot, cols_hot, weighted, grid_sum, tall, wide, green, left, mid, line, pot,
    recv1, send2, recv2, send3, recv3, send4, recv4, sends, recvs, green_sem,
):
    me = lax.axis_index("grp") * slab + lax.axis_index("slab")
    half = devices

    def place(k):
        p = lax.rem(me + k, devices)
        return p, (p // slab, lax.rem(p, slab))

    barrier = pltpu.get_barrier_semaphore()

    def greet(k, carry):
        pl.semaphore_signal(barrier, inc=1, device_id=place(k)[1], device_id_type=pl.DeviceIdType.MESH)
        return carry

    lax.fori_loop(1, devices, greet, 0)
    green_copy = pltpu.make_async_copy(green_hbm, green, green_sem)
    green_copy.start()

    for h in range(2):
        lanes = slice(h * LANES, (h + 1) * LANES)
        tall[0, :, lanes], tall[1, :, lanes] = halves(table[h])
        for j in range(4):
            block = table.at[h][pl.ds(j, half, stride=4), :]
            rows = slice(j * half, (j + 1) * half)
            tall[2, rows, lanes], tall[3, rows, lanes] = halves(block)
            wide[0, lanes, rows], wide[1, lanes, rows] = halves(block.T)
    for q in range(4):
        lanes = slice(q * LANES, (q + 1) * LANES)
        for xx in range(2):
            block = table_t.at[q][pl.ds(xx, half, stride=2), :]
            rows = slice(xx * half, (xx + 1) * half)
            wide[2, rows, lanes], wide[3, rows, lanes] = halves(block)
            tall[4, lanes, rows], tall[5, lanes, rows] = halves(block.T)

    pl.semaphore_wait(barrier, devices - 1)

    def row_of(ref, p):
        return ref.at[p]

    def tile_of(ref, p):
        return ref.at[:, pl.ds(pl.multiple_of(p * 8, 8), 8), :]

    def start_all(number, source, target, view):
        def start(k, carry):
            p, where = place(k)
            pltpu.make_async_remote_copy(
                src_ref=view(source, p), dst_ref=view(target, me),
                send_sem=sends.at[number], recv_sem=recvs.at[number],
                device_id=where, device_id_type=pl.DeviceIdType.MESH,
            ).start()
            return carry

        lax.fori_loop(1, devices, start, 0)

    def wait_all(ref, sem, view):
        part = ref.at[pl.ds(0, devices - 1)] if view is row_of else ref.at[:, pl.ds(0, (devices - 1) * 8), :]
        pltpu.make_async_copy(part, part, sem).wait()

    start_all(0, values, recv1, row_of)
    recv1[me] = values[me]

    row_id = lax.broadcasted_iota(jnp.int32, (2 * GY, LANES), 0)
    col_id = lax.broadcasted_iota(jnp.int32, (GZ, LANES), 0)

    def mark(e, carry):
        c = e // 8
        lanes = pl.ds(pl.multiple_of(lax.rem(e, 8) * LANES, LANES), LANES)
        cell = cells[e]
        row = lax.shift_right_logical(cell, 8)
        col = lax.bitwise_and(cell, 255)
        rows_hot[c, :, lanes] = jnp.where(row_id == row, 1.0, 0.0).astype(jnp.bfloat16)
        cols_hot[c, :, lanes] = jnp.where(col_id == col, 1.0, 0.0).astype(jnp.bfloat16)
        return carry

    lax.fori_loop(0, devices, mark, 0)
    wait_all(recv1, recvs.at[0], row_of)

    grid_sum[...] = jnp.zeros_like(grid_sum)

    def spread(c, carry):
        for k in range(8):
            lanes = slice(k * LANES, (k + 1) * LANES)
            hot = cols_hot[c, :, lanes]
            top, rest = halves(jnp.broadcast_to(recv1[c * 8 + k], (GZ, LANES)))
            weighted[0:GZ, lanes] = hot * top
            weighted[GZ:, lanes] = hot * rest
        grid_sum[...] += lax.dot_general(weighted[...], rows_hot[c], NT, preferred_element_type=jnp.float32)
        return carry

    lax.fori_loop(0, devices // 8, spread, 0)

    for xx in range(2):
        part = slice(xx * GY, (xx + 1) * GY)
        grid = halves(grid_sum[0:GZ, part] + grid_sum[GZ:, part])
        for j in range(4):
            rows = slice(j * half, (j + 1) * half)
            planes = product((tall[2, rows], tall[3, rows]), grid, NN)
            for h in range(2):
                send2.at[h][pl.ds(2 * j + xx, half, stride=8), :] = planes[:, h * LANES:(h + 1) * LANES]

    start_all(1, send2, recv2, tile_of)
    mine = pl.ds(pl.multiple_of(me * 8, 8), 8)
    recv2[:, mine, :] = send2[:, mine, :]
    green_copy.wait()
    wait_all(recv2, recvs.at[1], tile_of)

    for j in range(4):
        for h in range(2):
            lanes = slice(h * LANES, (h + 1) * LANES)
            for xx in range(2):
                rows = slice(xx * half, (xx + 1) * half)
                piece = recv2.at[h][pl.ds(2 * j + xx, half, stride=8), :]
                left[0, rows, lanes], left[1, rows, lanes] = halves(piece)
        line[...] = jnp.zeros_like(line)

        def convolve(b, carry):
            rows = pl.ds(pl.multiple_of(b * 256, 256), 256)
            along_x = halves(product((tall[4, rows], tall[5, rows]), (left[0], left[1]), NN))
            spectral = product(along_x, (tall[0], tall[1]), NT)
            scaled = halves(spectral * green[j, rows, :])
            back_y = halves(product(scaled, (tall[0], tall[1]), NN))
            line[...] += product((wide[2, :, rows], wide[3, :, rows]), back_y, NN)
            return carry

        lax.fori_loop(0, 2, convolve, 0)
        for h in range(2):
            for xx in range(2):
                send3.at[h][pl.ds(2 * j + xx, half, stride=8), :] = line[xx * half:(xx + 1) * half, h * LANES:(h + 1) * LANES]

    start_all(2, send3, recv3, tile_of)
    recv3[:, mine, :] = send3[:, mine, :]
    wait_all(recv3, recvs.at[2], tile_of)

    scale = 1.0 / float(8 * GX * GY * GZ)
    for xx in range(2):
        for j in range(4):
            rows = slice(j * half, (j + 1) * half)
            for h in range(2):
                lanes = slice(h * LANES, (h + 1) * LANES)
                piece = recv3.at[h][pl.ds(2 * j + xx, half, stride=8), :]
                mid[0, rows, lanes], mid[1, rows, lanes] = halves(piece)
        top, rest = halves(product((wide[0], wide[1]), (mid[0], mid[1]), NN) * scale)
        part = slice(xx * GY, (xx + 1) * GY)
        pot[0:GZ, part] = top
        pot[GZ:, part] = rest

    def sample(c, carry):
        for k in range(4):
            lanes = slice(k * 256, (k + 1) * 256)
            read = lax.dot_general(pot[...], rows_hot[c, :, lanes], NN, preferred_element_type=jnp.float32)
            kept = (read[0:GZ] + read[GZ:]) * cols_hot[c, :, lanes].astype(jnp.float32)
            total = jnp.sum(kept, axis=0, keepdims=True)
            for i in range(2):
                send4[c * 8 + 2 * k + i] = total[:, i * LANES:(i + 1) * LANES]
        return carry

    lax.fori_loop(0, devices // 8, sample, 0)

    start_all(3, send4, recv4, row_of)
    recv4[me] = send4[me]
    wait_all(recv4, recvs.at[3], row_of)
    out[...] = recv4[...]
    for number, (ref, view) in enumerate(((values, row_of), (send2, tile_of), (send3, tile_of), (send4, row_of))):
        wait_all(ref, sends.at[number], view)


def far_grid(outgoing, stencil_cells, green_spectrum, devices, slab):
    table = cas_table(2 * GZ, GZ, 2 * GZ)
    vmem = pl.BlockSpec(memory_space=pltpu.VMEM)
    f32, bf16 = jnp.float32, jnp.bfloat16
    rows = devices * 8
    return pl.pallas_call(
        functools.partial(whole_kernel, devices, slab),
        out_shape=jax.ShapeDtypeStruct((devices, 1, LANES), f32),
        in_specs=[vmem, vmem, vmem, vmem, pl.BlockSpec(memory_space=pl.ANY)],
        out_specs=vmem,
        scratch_shapes=[
            pltpu.VMEM((devices // 8, 2 * GY, 8 * LANES), bf16),
            pltpu.VMEM((devices // 8, GZ, 8 * LANES), bf16),
            pltpu.VMEM((2 * GZ, 8 * LANES), bf16),
            pltpu.VMEM((2 * GZ, 2 * GY), f32),
            pltpu.VMEM((6, 2 * GZ, GZ), bf16),
            pltpu.VMEM((4, GZ, 2 * GZ), bf16),
            pltpu.VMEM((4, 2 * GX, 2 * GY), f32),
            pltpu.VMEM((2, GX, GY), bf16),
            pltpu.VMEM((2, 2 * GZ, GY), bf16),
            pltpu.VMEM((GX, GY), f32),
            pltpu.VMEM((2 * GZ, 2 * GY), bf16),
            pltpu.VMEM((devices, 1, LANES), f32),
            pltpu.VMEM((2, rows, LANES), f32),
            pltpu.VMEM((2, rows, LANES), f32),
            pltpu.VMEM((2, rows, LANES), f32),
            pltpu.VMEM((2, rows, LANES), f32),
            pltpu.VMEM((devices, 1, LANES), f32),
            pltpu.VMEM((devices, 1, LANES), f32),
            pltpu.SemaphoreType.DMA((4,)),
            pltpu.SemaphoreType.DMA((4,)),
            pltpu.SemaphoreType.DMA,
        ],
        compiler_params=pltpu.CompilerParams(
            collective_id=0, has_side_effects=True, vmem_limit_bytes=58 * 1024 * 1024
        ),
    )(outgoing, stencil_cells, jnp.asarray(lane_parts(table)), jnp.asarray(lane_parts(table.T)), green_spectrum)


def per_device(
    charges,
    projection,
    stencil_block,
    stencil_dest,
    stencil_cells,
    green_spectrum,
    near_blocks,
    near_target,
    near_source,
):
    devices = lax.axis_size(("grp", "slab"))
    sblocks = stencil_block.shape[0]
    capacity = stencil_cells.shape[0] // devices
    panel_rows = charges.reshape(-1, BLK)
    pblocks = panel_rows.shape[0]
    owning = one_hot_rows(stencil_block, pblocks)
    gathered = jnp.dot(owning, panel_rows, precision=highest)
    values = jnp.einsum("bsp,bp->bs", projection, gathered, precision=highest)
    target = stencil_dest[:, 0]
    matches = one_hot_rows(target, devices)
    triangle = (jnp.arange(sblocks)[:, None] >= jnp.arange(sblocks)[None, :]).astype(jnp.float32)
    running = jnp.dot(triangle, matches, precision=highest)
    ranking = (jnp.sum(running * matches, axis=1) - 1.0).astype(jnp.int32)
    position = target * capacity + ranking
    placing = (
        jnp.arange(devices * capacity, dtype=jnp.int32)[:, None] == position[None, :]
    ).astype(jnp.float32)
    outgoing = jnp.dot(placing, values, precision=highest).reshape(devices, 1, capacity * STEN)
    cell_rows = stencil_cells.reshape(devices, 1, capacity * STEN)
    slab = lax.axis_size("slab")
    returned = far_grid(outgoing, cell_rows, green_spectrum, devices, slab).reshape(devices * capacity, STEN)
    at_stencil = lax.dot_general(placing, returned, (((0,), (0,)), ((), ())), precision=highest)
    far_terms = jnp.einsum("bsp,bs->bp", projection, at_stencil, precision=highest)
    far_field = lax.dot_general(owning, far_terms, (((0,), (0,)), ((), ())), precision=highest)
    extended = with_halo(charges, ((("grp", "slab"), 0),), charges.shape[0]).reshape(-1, BLK)
    sources = jnp.dot(one_hot_rows(near_source, extended.shape[0]), extended, precision=highest)
    near_terms = jnp.einsum("nij,nj->ni", near_blocks, sources, precision=highest)
    receiver = (jnp.arange(pblocks, dtype=jnp.int32)[:, None] == near_target[None, :]).astype(
        jnp.float32
    )
    near_field = jnp.dot(receiver, near_terms, precision=highest)
    return (far_field + near_field).reshape(-1)


def solution(mesh):
    placed = (
        P(("grp", "slab")),
        P(("grp", "slab"), None, None),
        P(("grp", "slab")),
        P(("grp", "slab"), None),
        P(("grp", "slab"), None),
        P(("grp", "slab"), None, None),
        P(("grp", "slab"), None, None),
        P(("grp", "slab")),
        P(("grp", "slab")),
    )
    return jax.shard_map(
        per_device, mesh=mesh, in_specs=placed, out_specs=P(("grp", "slab")), check_vma=False
    )
```

profile of v0, /device:TPU:1, one launch (start us, length us, event | category | flops | bytes accessed | tf_op | source)
XLA Modules:
  0.0 156.6 jit_solution(10780158113631107997)
XLA Ops:
  0.0 3.4 %collective-permute-start.1 = (f32[4096]{0:T(1024)}, f32[4096]{0:T(1024)S(1)}, u32[]{:S(2)}, u32[]{:S(2)}) collective-permute-start(f32[4096]{0:T(1024)} %param.11), channel_id=1, source_target_pairs={{1,0},{2,1},{3,2},{4,3},{5,4},{6,5},{7,6},{8,7},{9,8},{10,9},{11,1... | collective-permute-start | bytes 49160 | tf_op jit(solution)/shard_map/ppermute | solution.py:33
  3.4 3.1 %collective-permute-start = (f32[4096]{0:T(1024)}, f32[4096]{0:T(1024)S(1)}, u32[]{:S(2)}, u32[]{:S(2)}) collective-permute-start(f32[4096]{0:T(1024)} %param.11), channel_id=1, source_target_pairs={{0,1},{1,2},{2,3},{3,4},{4,5},{5,6},{6,7},{7,8},{8,9},{9,10},{10,1... | collective-permute-start | bytes 49160 | tf_op jit(solution)/shard_map/ppermute | solution.py:32
  6.6 0.8 reshape.32
  7.4 0.9 fusion
  8.3 0.7 convert_add_fusion
  8.9 0.9 copy.15
  9.9 0.7 reshape.34
  10.6 5.6 %copy.23 = f32[128,64,64]{2,1,0:T(8,128)} copy(f32[128,64,64]{0,2,1:T(8,128)} %param.12) | data formatting | bytes 4194304 | tf_op args[1]
  16.2 0.2 fusion.13
  16.4 8.3 %fusion.19 = f32[128,1,64]{2,1,0:T(1,128)S(1)} fusion(f32[128,64,1]{1,2,0:T(1,128)S(1)} %bitcast.37, f32[128,64,64]{2,1,0:T(8,128)} %copy.23), kind=kOutput, calls=%fused_computation.28 | convolution fusion | flops 6291456 | bytes 2162688 | tf_op jit(solution)/shard_map/bsp,bp->bs/dot_general | solution.py:290
  24.7 0.2 fusion.4
  24.9 0.7 reshape.33
  25.6 102.5 %shard_map.109 = f32[128,1,128]{2,1,0:T(1,128)} custom-call(f32[128,1,128]{2,1,0:T(1,128)} %bitcast.33, s32[128,1,128]{2,1,0:T(1,128)} %bitcast.32, f32[2,512,128]{2,1,0:T(8,128)} %constant.12.clone.table, f32[4,256,128]{2,1,0:T(8,128)} %constant.13.clone.table_t, f32[4,512,512]{2,1,0:T(8,128)} %green_hbm.1), custom_call_target="tpu_custom_call" | custom-call | tf_op jit(solution)/shard_map/pallas_call | solution.py:238
  128.2 0.5 broadcast.24
  128.7 1.6 %reduce.3 = f32[128,128]{1,0:T(8,128)S(1)} reduce(f32[128,1,128]{2,1,0:T(1,128)} %shard_map.109, f32[]{:T(128)} %broadcast.24), dimensions={1}, to_apply=%pallas_call.3.reduce_sub_computation.3 | reduce | bytes 131076 | tf_op jit(solution)/shard_map/pallas_call | solution.py:238
  130.3 0.1 reshape.35
  130.4 0.3 fusion.3
  130.7 5.5 %fusion.20 = f32[128,1,64]{2,1,0:T(1,128)S(1)} fusion(f32[128,64,1]{1,2,0:T(1,128)S(1)} %bitcast.34, f32[128,64,64]{2,1,0:T(8,128)} %copy.23), kind=kOutput, calls=%fused_computation.29 | convolution fusion | flops 6291456 | bytes 2162688 | tf_op jit(solution)/shard_map/bsp,bs->bp/dot_general | solution.py:305
  136.2 0.3 fusion.12
  136.5 9.3 %copy.26 = f32[256,64,64]{1,2,0:T(8,128)} copy(f32[256,64,64]{0,2,1:T(8,128)} %param.17) | data formatting | bytes 8388608 | tf_op args[6]
  145.9 0.3 fusion.1
  146.3 9.5 %fusion.21 = f32[256,1,64]{2,1,0:T(1,128)S(1)} fusion(f32[256,64,1]{1,2,0:T(1,128)S(1)} %bitcast.30, f32[256,64,64]{1,2,0:T(8,128)} %copy.26), kind=kOutput, calls=%fused_computation.30 | convolution fusion | flops 12582912 | bytes 4325376 | tf_op jit(solution)/shard_map/nij,nj->ni/dot_general | solution.py:309
  155.8 0.2 convolution_add_fusion
  155.9 0.7 reshape.36
  (10 shorter events, 0.2 us)
Async XLA Ops:
  0.0 16.2 %copy-start = (s32[128]{0:T(128)S(1)}, s32[128]{0:T(128)}, u32[]{:S(2)}) copy-start(s32[128]{0:T(128)} %param.13) | copy-start | bytes 1540
  0.0 145.8 %collective-permute-start.1 = (f32[4096]{0:T(1024)}, f32[4096]{0:T(1024)S(1)}, u32[]{:S(2)}, u32[]{:S(2)}) collective-permute-start(f32[4096]{0:T(1024)} %param.11), channel_id=1, source_target_pairs={{1,0},{2,1},{3,2},{4,3},{5,4},{6,5},{7,6},{8,7},{9,8},{10,9},{11,1... | collective-permute-start | bytes 49160 | tf_op jit(solution)/shard_map/ppermute | solution.py:33
  3.4 142.4 %collective-permute-start = (f32[4096]{0:T(1024)}, f32[4096]{0:T(1024)S(1)}, u32[]{:S(2)}, u32[]{:S(2)}) collective-permute-start(f32[4096]{0:T(1024)} %param.11), channel_id=1, source_target_pairs={{0,1},{1,2},{2,3},{3,4},{4,5},{5,6},{6,7},{7,8},{8,9},{9,10},{10,1... | collective-permute-start | bytes 49160 | tf_op jit(solution)/shard_map/ppermute | solution.py:32
  136.5 9.4 %copy-start.1 = (s32[256]{0:T(256)S(1)}, s32[256]{0:T(256)}, u32[]{:S(2)}) copy-start(s32[256]{0:T(256)} %param.19) | copy-start | bytes 3076
  146.2 9.5 %copy-start.2 = (s32[256]{0:T(256)S(1)}, s32[256]{0:T(256)}, u32[]{:S(2)}) copy-start(s32[256]{0:T(256)} %param.18) | copy-start | bytes 3076
where the time goes:
time: 157 us
  Pallas kernels  103 us (66%)
  matrix products  25.7 us (16%)
  local copies, waits for them, and re-layouts  19.4 us (12%)
  starting transfers between devices  6.54 us (4%)
  other arithmetic  2.31 us (1%)
    pallas_call x1, Pallas kernels, far_grid(): pl.pallas_call(functools.partial(whole_kernel, devices, slab), out_shape=...  103 us
    unnamed x9, local copies, waits for them, and re-layouts  15.8 us
    dot_general x1, matrix products, per_device(): jnp.einsum('nij,nj->ni', near_blocks, sources, precision=highest)  9.48 us
    dot_general x1, matrix products, per_device(): values = jnp.einsum('bsp,bp->bs', projection, gathered, precision=highest)  8.33 us
    dot_general x1, matrix products, per_device(): jnp.einsum('bsp,bs->bp', projection, at_stencil, precision=highest)  5.47 us
    ppermute x1, starting transfers between devices, with_halo(): after = lax.ppermute(first, axis, down)  3.41 us
  transfers between devices with their start and end apart: 2, of which 0 were waited for; matrix products, arithmetic and copies ran while one was open for 23% of the time, Pallas kernels for 65%

commit v1 on v0

v1 whole, which is shorter than its diff:
```python
import functools
import math

import jax
import jax.numpy as jnp
import numpy as np
from jax import lax
from jax.experimental import pallas as pl
from jax.experimental.pallas import tpu as pltpu
from jax.sharding import PartitionSpec as P

GX = 256
GY = 256
GZ = 256
BLK = 64
STEN = 64
LANES = 128


highest = lax.Precision.HIGHEST
NN = (((1,), (0,)), ((), ()))
NT = (((1,), (1,)), ((), ()))


def with_halo(x, sides, width):
    for axis, dim in sides:
        devices, length = (lax.axis_size(axis), x.shape[dim])
        up = [(i, (i + 1) % devices) for i in range(devices - 1)]
        down = [(j, i) for i, j in up]
        last = lax.slice_in_dim(x, length - width, length, axis=dim)
        first = lax.slice_in_dim(x, 0, width, axis=dim)
        before = lax.ppermute(last, axis, up)
        after = lax.ppermute(first, axis, down)
        x = jnp.concatenate([before, x, after], axis=dim)
    return x


def one_hot_rows(indices, count):
    return (indices[:, None] == jnp.arange(count, dtype=jnp.int32)[None, :]).astype(jnp.float32)


def cas_table(rows, columns, length):
    phase = np.outer(np.arange(rows), np.arange(columns)) % length * (2.0 * math.pi / length)
    return (np.cos(phase) + np.sin(phase)).astype(np.float32)


def lane_parts(table):
    return np.stack(np.split(table, table.shape[1] // LANES, axis=1))


def halves(x):
    top = x.astype(jnp.bfloat16)
    return top, (x - top.astype(jnp.float32)).astype(jnp.bfloat16)


def product(left, right, form):
    def one(a, b):
        return lax.dot_general(a, b, form, preferred_element_type=jnp.float32)

    return one(left[0], right[0]) + one(left[0], right[1]) + one(left[1], right[0])


def whole_kernel(
    devices, slab, values, cells, table, table_t, green_hbm, out,
    rows_hot, cols_hot, weighted, weighted_next, grid_sum, tall, wide, green, left, right, mid, pot,
    recv1, send2a, send2b, recv2a, recv2b, send3a, send3b, recv3a, recv3b, send4, recv4, sends, recvs, green_sem,
):
    send2, recv2, send3, recv3 = (send2a, send2b), (recv2a, recv2b), (send3a, send3b), (recv3a, recv3b)
    me = lax.axis_index("grp") * slab + lax.axis_index("slab")
    half = devices

    def place(k):
        p = lax.rem(me + k, devices)
        return p, (p // slab, lax.rem(p, slab))

    barrier = pltpu.get_barrier_semaphore()

    def greet(k, carry):
        pl.semaphore_signal(barrier, inc=1, device_id=place(k)[1], device_id_type=pl.DeviceIdType.MESH)
        return carry

    lax.fori_loop(1, devices, greet, 0)
    green_copy = pltpu.make_async_copy(green_hbm, green, green_sem)
    green_copy.start()

    for h in range(2):
        lanes = slice(h * LANES, (h + 1) * LANES)
        tall[0, :, lanes], tall[1, :, lanes] = halves(table[h])
        for j in range(4):
            block = table.at[h][pl.ds(j, half, stride=4), :]
            rows = slice(j * half, (j + 1) * half)
            tall[2, rows, lanes], tall[3, rows, lanes] = halves(block)
            wide[0, lanes, rows], wide[1, lanes, rows] = halves(block.T)
    for q in range(4):
        lanes = slice(q * LANES, (q + 1) * LANES)
        for xx in range(2):
            block = table_t.at[q][pl.ds(xx, half, stride=2), :]
            rows = slice(xx * half, (xx + 1) * half)
            wide[2, rows, lanes], wide[3, rows, lanes] = halves(block)
            tall[4, lanes, rows], tall[5, lanes, rows] = halves(block.T)

    pl.semaphore_wait(barrier, devices - 1)

    def row_of(ref, p):
        return ref.at[p]

    def tile_of(ref, p):
        return ref.at[pl.ds(pl.multiple_of(p * 8, 8), 8), :]

    def start_one(number, source, target, view, k):
        p, where = place(k)
        pltpu.make_async_remote_copy(
            src_ref=view(source, p), dst_ref=view(target, me),
            send_sem=sends.at[number], recv_sem=recvs.at[number],
            device_id=where, device_id_type=pl.DeviceIdType.MESH,
        ).start()

    def start_all(number, source, target):
        def start(k, carry):
            start_one(number, source, target, tile_of, k)
            return carry

        lax.fori_loop(1, devices, start, 0)

    def wait_all(ref, sem, view):
        part = ref.at[pl.ds(0, devices - 1)] if view is row_of else ref.at[pl.ds(0, (devices - 1) * 8), :]
        pltpu.make_async_copy(part, part, sem).wait()

    row_id = lax.broadcasted_iota(jnp.int32, (2 * GY, LANES), 0)
    col_id = lax.broadcasted_iota(jnp.int32, (GZ, LANES), 0)

    def mark(e):
        c = e // 8
        lanes = pl.ds(pl.multiple_of(lax.rem(e, 8) * LANES, LANES), LANES)
        cell = cells[e]
        row = lax.shift_right_logical(cell, 8)
        col = lax.bitwise_and(cell, 255)
        rows_hot[c, :, lanes] = jnp.where(row_id == row, 1.0, 0.0).astype(jnp.bfloat16)
        cols_hot[c, :, lanes] = jnp.where(col_id == col, 1.0, 0.0).astype(jnp.bfloat16)

    def send_and_mark(k, carry):
        start_one(0, values, recv1, row_of, k)
        mark(k)
        return carry

    lax.fori_loop(1, devices, send_and_mark, 0)
    mark(0)
    recv1[me] = values[me]
    wait_all(recv1, recvs.at[0], row_of)

    def weigh(c, into):
        for k in range(8):
            lanes = slice(k * LANES, (k + 1) * LANES)
            hot = cols_hot[c, :, lanes]
            top, rest = halves(jnp.broadcast_to(recv1[c * 8 + k], (GZ, LANES)))
            into[0:GZ, lanes] = hot * top
            into[GZ:, lanes] = hot * rest

    def add_chunk(c, weights):
        grid_sum[...] += lax.dot_general(weights[...], rows_hot[c], NT, preferred_element_type=jnp.float32)

    grid_sum[...] = jnp.zeros_like(grid_sum)
    weigh(0, weighted)
    chunks = devices // 8

    def spread(i, carry):
        weigh(2 * i + 1, weighted_next)
        add_chunk(2 * i, weighted)
        weigh(jnp.minimum(2 * i + 2, chunks - 1), weighted)
        add_chunk(2 * i + 1, weighted_next)
        return carry

    lax.fori_loop(0, chunks // 2, spread, 0)

    mine = pl.ds(pl.multiple_of(me * 8, 8), 8)

    def spots(j, xx, h):
        return pl.ds(4 * j + 2 * xx + h, half, stride=8)

    for xx in range(2):
        part = slice(xx * GY, (xx + 1) * GY)
        left[xx], right[xx] = halves(grid_sum[0:GZ, part] + grid_sum[GZ:, part])
    for side in range(2):
        for xx in range(2):
            for j in range(2):
                rows = slice((2 * side + j) * half, (2 * side + j + 1) * half)
                planes = product((tall[2, rows], tall[3, rows]), (left[xx], right[xx]), NN)
                for h in range(2):
                    send2[side][spots(j, xx, h), :] = planes[:, h * LANES:(h + 1) * LANES]
        start_all(1 + side, send2[side], recv2[side])
        recv2[side][mine, :] = send2[side][mine, :]
    green_copy.wait()

    for side in range(2):
        wait_all(recv2[side], recvs.at[1 + side], tile_of)
        for j in range(2):
            for h in range(2):
                lanes = slice(h * LANES, (h + 1) * LANES)
                for xx in range(2):
                    rows = slice(xx * half, (xx + 1) * half)
                    left[0, rows, lanes], left[1, rows, lanes] = halves(recv2[side][spots(j, xx, h), :])
            total = None
            for b in range(2):
                rows = slice(b * GX, (b + 1) * GX)
                along_x = halves(product((tall[4, rows], tall[5, rows]), (left[0], left[1]), NN))
                spectral = product(along_x, (tall[0], tall[1]), NT)
                scaled = halves(spectral * green[2 * side + j, rows, :])
                back_y = halves(product(scaled, (tall[0], tall[1]), NN))
                term = product((wide[2, :, rows], wide[3, :, rows]), back_y, NN)
                total = term if total is None else total + term
            for h in range(2):
                for xx in range(2):
                    send3[side][spots(j, xx, h), :] = total[xx * half:(xx + 1) * half, h * LANES:(h + 1) * LANES]
        start_all(3 + side, send3[side], recv3[side])
        recv3[side][mine, :] = send3[side][mine, :]

    for side in range(2):
        wait_all(recv3[side], recvs.at[3 + side], tile_of)
        for xx in range(2):
            for j in range(2):
                rows = slice((2 * side + j) * half, (2 * side + j + 1) * half)
                for h in range(2):
                    lanes = slice(xx * GY + h * LANES, xx * GY + (h + 1) * LANES)
                    mid[0, rows, lanes], mid[1, rows, lanes] = halves(recv3[side][spots(j, xx, h), :])
    scale = 1.0 / float(8 * GX * GY * GZ)
    for xx in range(2):
        part = slice(xx * GY, (xx + 1) * GY)
        top, rest = halves(product((wide[0], wide[1]), (mid[0, :, part], mid[1, :, part]), NN) * scale)
        pot[0:GZ, part] = top
        pot[GZ:, part] = rest

    def sample(i, carry):
        c = lax.rem(me // 8 + i, chunks)
        for k in range(4):
            lanes = slice(k * 256, (k + 1) * 256)
            read = lax.dot_general(pot[...], rows_hot[c, :, lanes], NN, preferred_element_type=jnp.float32)
            kept = (read[0:GZ] + read[GZ:]) * cols_hot[c, :, lanes].astype(jnp.float32)
            total = jnp.sum(kept, axis=0, keepdims=True)
            for q in range(2):
                send4[c * 8 + 2 * k + q] = total[:, q * LANES:(q + 1) * LANES]
        return carry

    def send_chunk(i):
        c = lax.rem(me // 8 + i, chunks)
        for q in range(8):
            p = c * 8 + q

            @pl.when(p != me)
            def _():
                start_one(5, send4, recv4, row_of, lax.rem(p + devices - me, devices))

    def sample_and_send(i, carry):
        sample(i, 0)
        send_chunk(i)
        return carry

    lax.fori_loop(0, chunks, sample_and_send, 0)
    recv4[me] = send4[me]
    wait_all(recv4, recvs.at[5], row_of)
    out[...] = recv4[...]
    wait_all(values, sends.at[0], row_of)
    for side in range(2):
        wait_all(send2[side], sends.at[1 + side], tile_of)
        wait_all(send3[side], sends.at[3 + side], tile_of)
    wait_all(send4, sends.at[5], row_of)


def far_grid(outgoing, stencil_cells, green_spectrum, devices, slab):
    table = cas_table(2 * GZ, GZ, 2 * GZ)
    vmem = pl.BlockSpec(memory_space=pltpu.VMEM)
    f32, bf16 = jnp.float32, jnp.bfloat16
    rows = devices * 8
    return pl.pallas_call(
        functools.partial(whole_kernel, devices, slab),
        out_shape=jax.ShapeDtypeStruct((devices, 1, LANES), f32),
        in_specs=[vmem, vmem, vmem, vmem, pl.BlockSpec(memory_space=pl.ANY)],
        out_specs=vmem,
        scratch_shapes=[
            pltpu.VMEM((devices // 8, 2 * GY, 8 * LANES), bf16),
            pltpu.VMEM((devices // 8, GZ, 8 * LANES), bf16),
            pltpu.VMEM((2 * GZ, 8 * LANES), bf16),
            pltpu.VMEM((2 * GZ, 8 * LANES), bf16),
            pltpu.VMEM((2 * GZ, 2 * GY), f32),
            pltpu.VMEM((6, 2 * GZ, GZ), bf16),
            pltpu.VMEM((4, GZ, 2 * GZ), bf16),
            pltpu.VMEM((4, 2 * GX, 2 * GY), f32),
            pltpu.VMEM((2, GX, GY), bf16),
            pltpu.VMEM((2, GX, GY), bf16),
            pltpu.VMEM((2, 2 * GZ, 2 * GY), bf16),
            pltpu.VMEM((2 * GZ, 2 * GY), bf16),
            pltpu.VMEM((devices, 1, LANES), f32),
            *[pltpu.VMEM((rows, LANES), f32)] * 8,
            pltpu.VMEM((devices, 1, LANES), f32),
            pltpu.VMEM((devices, 1, LANES), f32),
            pltpu.SemaphoreType.DMA((6,)),
            pltpu.SemaphoreType.DMA((6,)),
            pltpu.SemaphoreType.DMA,
        ],
        compiler_params=pltpu.CompilerParams(
            collective_id=0, has_side_effects=True, vmem_limit_bytes=48 * 1024 * 1024
        ),
    )(outgoing, stencil_cells, jnp.asarray(lane_parts(table)), jnp.asarray(lane_parts(table.T)), green_spectrum)


def per_device(
    charges,
    projection,
    stencil_block,
    stencil_dest,
    stencil_cells,
    green_spectrum,
    near_blocks,
    near_target,
    near_source,
):
    devices = lax.axis_size(("grp", "slab"))
    sblocks = stencil_block.shape[0]
    capacity = stencil_cells.shape[0] // devices
    panel_rows = charges.reshape(-1, BLK)
    pblocks = panel_rows.shape[0]
    owning = one_hot_rows(stencil_block, pblocks)
    gathered = jnp.dot(owning, panel_rows, precision=highest)
    values = jnp.sum(projection * gathered[:, None, :], axis=2)
    target = stencil_dest[:, 0]
    matches = one_hot_rows(target, devices)
    triangle = (jnp.arange(sblocks)[:, None] >= jnp.arange(sblocks)[None, :]).astype(jnp.float32)
    running = jnp.dot(triangle, matches, precision=highest)
    ranking = (jnp.sum(running * matches, axis=1) - 1.0).astype(jnp.int32)
    position = target * capacity + ranking
    placing = (
        jnp.arange(devices * capacity, dtype=jnp.int32)[:, None] == position[None, :]
    ).astype(jnp.float32)
    outgoing = jnp.dot(placing, values, precision=highest).reshape(devices, 1, capacity * STEN)
    cell_rows = stencil_cells.reshape(devices, 1, capacity * STEN)
    slab = lax.axis_size("slab")
    returned = far_grid(outgoing, cell_rows, green_spectrum, devices, slab).reshape(devices * capacity, STEN)
    at_stencil = lax.dot_general(placing, returned, (((0,), (0,)), ((), ())), precision=highest)
    far_terms = jnp.sum(projection * at_stencil[:, :, None], axis=1)
    far_field = lax.dot_general(owning, far_terms, (((0,), (0,)), ((), ())), precision=highest)
    extended = with_halo(charges, ((("grp", "slab"), 0),), charges.shape[0]).reshape(-1, BLK)
    sources = jnp.dot(one_hot_rows(near_source, extended.shape[0]), extended, precision=highest)
    near_terms = jnp.sum(near_blocks * sources[:, None, :], axis=2)
    receiver = (jnp.arange(pblocks, dtype=jnp.int32)[:, None] == near_target[None, :]).astype(
        jnp.float32
    )
    near_field = jnp.dot(receiver, near_terms, precision=highest)
    return (far_field + near_field).reshape(-1)


def solution(mesh):
    placed = (
        P(("grp", "slab")),
        P(("grp", "slab"), None, None),
        P(("grp", "slab")),
        P(("grp", "slab"), None),
        P(("grp", "slab"), None),
        P(("grp", "slab"), None, None),
        P(("grp", "slab"), None, None),
        P(("grp", "slab")),
        P(("grp", "slab")),
    )
    return jax.shard_map(
        per_device, mesh=mesh, in_specs=placed, out_specs=P(("grp", "slab")), check_vma=False
    )
```

time: 157 us -> 108 us (0.69)
  matrix products: 25.7 us -> 3.09 us
  Pallas kernels: 103 us -> 87 us
  local copies, waits for them, and re-layouts: 19.4 us -> 4.68 us
  other arithmetic: 2.31 us -> 6.45 us
    dot_general x3 -> x0, matrix products: 23.3 us -> none  [the longest x1 9.48 us: per_device(): jnp.einsum('nij,nj->ni', near_blocks, sources, precision=highest)]
    pallas_call x1, Pallas kernels: 103 us -> 87 us  [far_grid(): pl.pallas_call(functools.partial(whole_kernel, devices, slab), out_shape=...]
    unnamed x9 -> x17, local copies, waits for them, and re-layouts: 15.8 us -> 2.31 us
    reduce_sum x0 -> x3, other arithmetic: none -> 4.98 us  [the longest x1 2.84 us: per_device(): near_terms = jnp.sum(near_blocks * sources[:, None, :], axis=2)]
  transfers between devices with their start and end apart: 2 -> 2, of which waited for: 0 -> 0; matrix products, arithmetic and copies ran while one was open for 23% -> 7% of each run, Pallas kernels for 65% -> 81%
where the time goes in v1:
time: 108 us
  Pallas kernels  87 us (81%)
  starting transfers between devices  6.55 us (6%)
  other arithmetic  6.45 us (6%)
  local copies, waits for them, and re-layouts  4.68 us (4%)
  matrix products  3.09 us (3%)
    pallas_call x1, Pallas kernels, far_grid(): pl.pallas_call(functools.partial(whole_kernel, devices, slab), out_shape=...  87 us
    ppermute x1, starting transfers between devices, with_halo(): before = lax.ppermute(last, axis, up)  4.63 us
    reduce_sum x1, other arithmetic, per_device(): near_terms = jnp.sum(near_blocks * sources[:, None, :], axis=2)  2.84 us
    unnamed x17, local copies, waits for them, and re-layouts  2.31 us
  transfers between devices with their start and end apart: 2, of which 0 were waited for; matrix products, arithmetic and copies ran while one was open for 7% of the time, Pallas kernels for 81%

profile of v1, /device:TPU:1, one launch (start us, length us, event | category | flops | bytes accessed | tf_op | source)
XLA Modules:
  0.0 108.0 jit_solution(8803157865360439121)
XLA Ops:
  0.0 4.6 %collective-permute-start = (f32[4096]{0:T(1024)}, f32[4096]{0:T(1024)S(1)}, u32[]{:S(2)}, u32[]{:S(2)}) collective-permute-start(f32[4096]{0:T(1024)} %param.11), channel_id=1, source_target_pairs={{0,1},{1,2},{2,3},{3,4},{4,5},{5,6},{6,7},{7,8},{8,9},{9,10},{10,1... | collective-permute-start | bytes 49160 | tf_op jit(solution)/shard_map/ppermute | solution.py:32
  4.6 1.9 %collective-permute-start.1 = (f32[4096]{0:T(1024)}, f32[4096]{0:T(1024)S(1)}, u32[]{:S(2)}, u32[]{:S(2)}) collective-permute-start(f32[4096]{0:T(1024)} %param.11), channel_id=1, source_target_pairs={{1,0},{2,1},{3,2},{4,3},{5,4},{6,5},{7,6},{8,7},{9,8},{10,9},{11,1... | collective-permute-start | bytes 49160 | tf_op jit(solution)/shard_map/ppermute | solution.py:33
  6.6 0.8 reshape.35
  7.4 0.9 fusion
  8.3 0.7 convert_add_fusion
  8.9 0.9 fusion.13
  9.9 1.9 %multiply_reduce_fusion.2 = f32[128,64]{0,1:T(8,128)S(1)} fusion(f32[128,64,64]{0,2,1:T(8,128)} %param.12, f32[128,64]{0,1:T(8,128)S(1)} %fusion.13), kind=kLoop, calls=%fused_computation.2 | loop fusion | flops 1040384 | bytes 2162688 | tf_op jit(solution)/shard_map/reduce_sum | solution.py:323
  11.8 0.2 fusion.4
  12.0 0.1 reshape.36
  12.1 0.1 copy.19
  12.2 0.1 reshape.37
  12.3 2.2 %copy-done = f32[4,512,512]{2,1,0:T(8,128)S(1)} copy-done((f32[4,512,512]{2,1,0:T(8,128)S(1)}, f32[4,512,512]{2,1,0:T(8,128)}, u32[]{:S(2)}) %copy-start) | copy-done | bytes 4194328
  14.5 87.0 %shard_map.109 = f32[128,1,128]{2,1,0:T(1,128)S(1)} custom-call(f32[128,1,128]{2,1,0:T(1,128)S(1)} %bitcast.9, s32[128,1,128]{2,1,0:T(1,128)S(1)} %bitcast.10, f32[2,512,128]{2,1,0:T(8,128)S(1)} %copy-done.1, f32[4,256,128]{2,1,0:T(8,128)S(1)} %copy-done.2, f32[4,512,512]{2,1,0:T(8,128)S(1)} %copy-done), custom_call_target="tpu_custom_call" | custom-call | tf_op jit(solution)/shard_map/pallas_call | solution.py:273
  101.5 0.5 broadcast.27
  102.0 0.8 reduce.3
  102.9 0.1 reshape.38
  102.9 0.3 fusion.3
  103.2 0.2 multiply_reduce_fusion.1
  103.4 0.1 concatenate.8
  103.6 0.3 fusion.1
  104.0 2.8 %multiply_reduce_fusion = f32[256,64]{0,1:T(8,128)S(1)} fusion(f32[256,64,64]{0,2,1:T(8,128)} %param.17, f32[256,64]{0,1:T(8,128)S(1)} %fusion.1), kind=kLoop, calls=%fused_computation | loop fusion | flops 2080768 | bytes 4325376 | tf_op jit(solution)/shard_map/reduce_sum | solution.py:342
  106.8 0.2 fusion.14
  107.0 0.3 convolution_add_fusion
  107.3 0.7 reshape.39
  (18 shorter events, 0.1 us)
Async XLA Ops:
  0.0 12.3 %copy-start.1 = (f32[2,512,128]{2,1,0:T(8,128)S(1)}, f32[2,512,128]{2,1,0:T(8,128)}, u32[]{:S(2)}) copy-start(f32[2,512,128]{2,1,0:T(8,128)} %constant.12.clone.table) | copy-start | bytes 1572868
  0.0 12.3 %copy-start.2 = (f32[4,256,128]{2,1,0:T(8,128)S(1)}, f32[4,256,128]{2,1,0:T(8,128)}, u32[]{:S(2)}) copy-start(f32[4,256,128]{2,1,0:T(8,128)} %constant.13.clone.table_t) | copy-start | bytes 1572868
  0.0 12.1 %copy-start.4 = (s32[256,64]{0,1:T(8,128)S(1)}, s32[256,64]{0,1:T(8,128)}, u32[]{:S(2)}) copy-start(s32[256,64]{0,1:T(8,128)} %param.15) | copy-start | bytes 196612
  0.0 103.4 %collective-permute-start = (f32[4096]{0:T(1024)}, f32[4096]{0:T(1024)S(1)}, u32[]{:S(2)}, u32[]{:S(2)}) collective-permute-start(f32[4096]{0:T(1024)} %param.11), channel_id=1, source_target_pairs={{0,1},{1,2},{2,3},{3,4},{4,5},{5,6},{6,7},{7,8},{8,9},{9,10},{10,1... | collective-permute-start | bytes 49160 | tf_op jit(solution)/shard_map/ppermute | solution.py:32
  4.6 98.9 %collective-permute-start.1 = (f32[4096]{0:T(1024)}, f32[4096]{0:T(1024)S(1)}, u32[]{:S(2)}, u32[]{:S(2)}) collective-permute-start(f32[4096]{0:T(1024)} %param.11), channel_id=1, source_target_pairs={{1,0},{2,1},{3,2},{4,3},{5,4},{6,5},{7,6},{8,7},{9,8},{10,9},{11,1... | collective-permute-start | bytes 49160 | tf_op jit(solution)/shard_map/ppermute | solution.py:33
  12.3 2.2 %copy-start = (f32[4,512,512]{2,1,0:T(8,128)S(1)}, f32[4,512,512]{2,1,0:T(8,128)}, u32[]{:S(2)}) copy-start(f32[4,512,512]{2,1,0:T(8,128)} %green_hbm.1) | copy-start | bytes 12582916
  14.5 88.7 %copy-start.3 = (f32[128,64,64]{0,2,1:T(8,128)S(1)}, f32[128,64,64]{0,2,1:T(8,128)}, u32[]{:S(2)}) copy-start(f32[128,64,64]{0,2,1:T(8,128)} %param.12) | copy-start | bytes 6291460
  101.5 2.1 %copy-start.7 = (s32[256]{0:T(256)S(1)}, s32[256]{0:T(256)}, u32[]{:S(2)}) copy-start(s32[256]{0:T(256)} %param.19) | copy-start | bytes 3076
  103.9 2.9 %copy-start.6 = (s32[256]{0:T(256)S(1)}, s32[256]{0:T(256)}, u32[]{:S(2)}) copy-start(s32[256]{0:T(256)} %param.18) | copy-start | bytes 3076
  103.9 3.1 %copy-start.5 = (s32[128]{0:T(128)S(1)}, s32[128]{0:T(128)}, u32[]{:S(2)}) copy-start(s32[128]{0:T(128)} %param.13) | copy-start | bytes 1540

commit v2 on v1

--- a/solution.py
+++ b/solution.py
@@ -17,26 +17,8 @@
 LANES = 128
 
 
-highest = lax.Precision.HIGHEST
 NN = (((1,), (0,)), ((), ()))
 NT = (((1,), (1,)), ((), ()))
-
-
-def with_halo(x, sides, width):
-    for axis, dim in sides:
-        devices, length = (lax.axis_size(axis), x.shape[dim])
-        up = [(i, (i + 1) % devices) for i in range(devices - 1)]
-        down = [(j, i) for i, j in up]
-        last = lax.slice_in_dim(x, length - width, length, axis=dim)
-        first = lax.slice_in_dim(x, 0, width, axis=dim)
-        before = lax.ppermute(last, axis, up)
-        after = lax.ppermute(first, axis, down)
-        x = jnp.concatenate([before, x, after], axis=dim)
-    return x
-
-
-def one_hot_rows(indices, count):
-    return (indices[:, None] == jnp.arange(count, dtype=jnp.int32)[None, :]).astype(jnp.float32)
 
 
 def cas_table(rows, columns, length):
@@ -53,6 +35,38 @@
     return top, (x - top.astype(jnp.float32)).astype(jnp.bfloat16)
 
 
+def exact_pick(table, hot, form):
+    first = table.astype(jnp.bfloat16)
+    second, third = halves(table - first.astype(jnp.float32))
+    total = None
+    for part in (third, second, first):
+        term = lax.dot_general(part, hot, form, preferred_element_type=jnp.float32)
+        total = term if total is None else total + term
+    return total
+
+
+def as_bf16(mask):
+    return jnp.where(mask, 1.0, 0.0).astype(jnp.bfloat16)
+
+
+def rows_equal(count, indices):
+    return lax.broadcasted_iota(jnp.int32, (count, indices.shape[1]), 0) == indices
+
+
+def by_parity(pair, indices):
+    return jnp.where(lax.bitwise_and(indices, 1) == 0, pair[0:BLK], pair[BLK:])
+
+
+def to_panels(terms, indices):
+    odd = lax.bitwise_and(indices, 1)
+    pair = jnp.concatenate([jnp.where(odd == 0, terms, 0.0), jnp.where(odd == 1, terms, 0.0)], axis=0)
+    hot = as_bf16(rows_equal(32, lax.shift_right_logical(indices, 1)))
+    top, rest = halves(pair)
+    return lax.dot_general(hot, top, NT, preferred_element_type=jnp.float32) + lax.dot_general(
+        hot, rest, NT, preferred_element_type=jnp.float32
+    )
+
+
 def product(left, right, form):
     def one(a, b):
         return lax.dot_general(a, b, form, preferred_element_type=jnp.float32)
@@ -61,9 +75,12 @@
 
 
 def whole_kernel(
-    devices, slab, values, cells, table, table_t, green_hbm, out,
+    devices, slab, charges, block, target, near_target, near_source, cells_t, table, table_t,
+    projection_hbm, near_hbm, green_hbm, out,
     rows_hot, cols_hot, weighted, weighted_next, grid_sum, tall, wide, green, left, right, mid, pot,
-    recv1, send2a, send2b, recv2a, recv2b, send3a, send3b, recv3a, recv3b, send4, recv4, sends, recvs, green_sem,
+    recv1, send2a, send2b, recv2a, recv2b, send3a, send3b, recv3a, recv3b, send4, recv4,
+    projection, near, halo, turned, cells, square, values, member, terms, sums,
+    sends, recvs, halo_sends, halo_recvs, load_sems,
 ):
     send2, recv2, send3, recv3 = (send2a, send2b), (recv2a, recv2b), (send3a, send3b), (recv3a, recv3b)
     me = lax.axis_index("grp") * slab + lax.axis_index("slab")
@@ -80,26 +97,61 @@
         return carry
 
     lax.fori_loop(1, devices, greet, 0)
-    green_copy = pltpu.make_async_copy(green_hbm, green, green_sem)
-    green_copy.start()
+    loads = [
+        pltpu.make_async_copy(source, into, load_sems.at[i])
+        for i, (source, into) in enumerate(((projection_hbm, projection), (near_hbm, near), (green_hbm, green)))
+    ]
+    for load in loads:
+        load.start()
+
+    turned[:, 0:STEN] = cells_t[...].T
+    cells[...] = jnp.concatenate([turned[pl.ds(i, half, stride=2), 0:STEN] for i in range(2)], axis=1)
+
+    hot = as_bf16(rows_equal(32, lax.shift_right_logical(block[...], 1)))
+    gathered = by_parity(exact_pick(charges[...].T, hot, NN), block[...])
+    loads[0].wait()
+    for s in range(STEN):
+        terms[s:s + 1, :] = jnp.sum(projection[s] * gathered, axis=0, keepdims=True)
+    named = rows_equal(devices, target[...])
+    named_hot = as_bf16(named)
+    across = (devices, devices)
+    earlier = as_bf16(lax.broadcasted_iota(jnp.int32, across, 0) < lax.broadcasted_iota(jnp.int32, across, 1))
+    before = lax.dot_general(named_hot, earlier, NN, preferred_element_type=jnp.float32)
+    member[0] = as_bf16(named & (before < 0.5))
+    member[1] = as_bf16(named & (before > 0.5))
+    empty = jnp.zeros((STEN, devices), jnp.bfloat16)
+    outgoing = jnp.zeros((devices, 2 * STEN), jnp.float32)
+    for part in halves(terms[0:STEN]):
+        for slot in range(2):
+            spread_part = jnp.concatenate([part, empty] if slot == 0 else [empty, part], axis=0)
+            outgoing += lax.dot_general(member[slot], spread_part, NT, preferred_element_type=jnp.float32)
+    square[...] = outgoing
+    for d in range(devices):
+        values[d] = square[d:d + 1, :]
 
     for h in range(2):
         lanes = slice(h * LANES, (h + 1) * LANES)
         tall[0, :, lanes], tall[1, :, lanes] = halves(table[h])
         for j in range(4):
-            block = table.at[h][pl.ds(j, half, stride=4), :]
+            chunk = table.at[h][pl.ds(j, half, stride=4), :]
             rows = slice(j * half, (j + 1) * half)
-            tall[2, rows, lanes], tall[3, rows, lanes] = halves(block)
-            wide[0, lanes, rows], wide[1, lanes, rows] = halves(block.T)
+            tall[2, rows, lanes], tall[3, rows, lanes] = halves(chunk)
+            wide[0, lanes, rows], wide[1, lanes, rows] = halves(chunk.T)
     for q in range(4):
         lanes = slice(q * LANES, (q + 1) * LANES)
         for xx in range(2):
-            block = table_t.at[q][pl.ds(xx, half, stride=2), :]
+            chunk = table_t.at[q][pl.ds(xx, half, stride=2), :]
             rows = slice(xx * half, (xx + 1) * half)
-            wide[2, rows, lanes], wide[3, rows, lanes] = halves(block)
-            tall[4, lanes, rows], tall[5, lanes, rows] = halves(block.T)
+            wide[2, rows, lanes], wide[3, rows, lanes] = halves(chunk)
+            tall[4, lanes, rows], tall[5, lanes, rows] = halves(chunk.T)
 
     pl.semaphore_wait(barrier, devices - 1)
+    halo_copies = []
+    for i, k in enumerate((1, devices - 1)):
+        halo_copies.append(pltpu.make_async_remote_copy(
+            src_ref=charges, dst_ref=halo.at[i], send_sem=halo_sends.at[i], recv_sem=halo_recvs.at[i],
+            device_id=place(k)[1], device_id_type=pl.DeviceIdType.MESH,
+        ))
 
     def row_of(ref, p):
         return ref.at[p]
@@ -132,7 +184,7 @@
     def mark(e):
         c = e // 8
         lanes = pl.ds(pl.multiple_of(lax.rem(e, 8) * LANES, LANES), LANES)
-        cell = cells[e]
+        cell = cells[pl.ds(e, 1), :]
         row = lax.shift_right_logical(cell, 8)
         col = lax.bitwise_and(cell, 255)
         rows_hot[c, :, lanes] = jnp.where(row_id == row, 1.0, 0.0).astype(jnp.bfloat16)
@@ -144,6 +196,8 @@
         return carry
 
     lax.fori_loop(1, devices, send_and_mark, 0)
+    for copy in halo_copies:
+        copy.start()
     mark(0)
     recv1[me] = values[me]
     wait_all(recv1, recvs.at[0], row_of)
@@ -189,7 +243,18 @@
                     send2[side][spots(j, xx, h), :] = planes[:, h * LANES:(h + 1) * LANES]
         start_all(1 + side, send2[side], recv2[side])
         recv2[side][mine, :] = send2[side][mine, :]
-    green_copy.wait()
+    for load in loads[1:]:
+        load.wait()
+    for copy in halo_copies:
+        copy.wait()
+
+    inside = [jnp.where(me > 0, halo[0], 0.0), charges[...], jnp.where(me < devices - 1, halo[1], 0.0)]
+    read = near_source[...]
+    near_hot = as_bf16(rows_equal(96, lax.shift_right_logical(read, 1)))
+    picked = by_parity(exact_pick(jnp.concatenate(inside, axis=0).T, near_hot, NN), read)
+    for i in range(BLK):
+        sums[i:i + 1, :] = jnp.sum(near[i] * picked, axis=0, keepdims=True)
+    panels = to_panels(sums[...], near_target[...])
 
     for side in range(2):
         wait_all(recv2[side], recvs.at[1 + side], tile_of)
@@ -257,7 +322,20 @@
     lax.fori_loop(0, chunks, sample_and_send, 0)
     recv4[me] = send4[me]
     wait_all(recv4, recvs.at[5], row_of)
-    out[...] = recv4[...]
+    for d in range(devices):
+        square[d:d + 1, :] = recv4[d]
+    returned = halves(square[...].T)
+    at_stencil = jnp.zeros((STEN, devices), jnp.float32)
+    for slot in range(2):
+        for part in returned:
+            at_stencil += lax.dot_general(
+                part[slot * STEN:(slot + 1) * STEN], member[slot], NN, preferred_element_type=jnp.float32
+            )
+    terms[...] = at_stencil
+    far = jnp.zeros((BLK, devices), jnp.float32)
+    for s in range(STEN):
+        far += projection[s] * terms[s:s + 1, :]
+    out[...] = panels + to_panels(far, block[...])
     wait_all(values, sends.at[0], row_of)
     for side in range(2):
         wait_all(send2[side], sends.at[1 + side], tile_of)
@@ -265,15 +343,31 @@
     wait_all(send4, sends.at[5], row_of)
 
 
-def far_grid(outgoing, stencil_cells, green_spectrum, devices, slab):
+def per_device(
+    slab,
+    devices,
+    charges,
+    projection,
+    stencil_block,
+    stencil_dest,
+    stencil_cells,
+    green_spectrum,
+    near_blocks,
+    near_target,
+    near_source,
+):
     table = cas_table(2 * GZ, GZ, 2 * GZ)
     vmem = pl.BlockSpec(memory_space=pltpu.VMEM)
+    whole = pl.BlockSpec(memory_space=pl.ANY)
     f32, bf16 = jnp.float32, jnp.bfloat16
     rows = devices * 8
-    return pl.pallas_call(
+    sblocks = stencil_block.shape[0]
+    nears = near_target.shape[0]
+    panels = (charges.shape[0] // LANES, LANES)
+    result = pl.pallas_call(
         functools.partial(whole_kernel, devices, slab),
-        out_shape=jax.ShapeDtypeStruct((devices, 1, LANES), f32),
-        in_specs=[vmem, vmem, vmem, vmem, pl.BlockSpec(memory_space=pl.ANY)],
+        out_shape=jax.ShapeDtypeStruct(panels, f32),
+        in_specs=[vmem] * 8 + [whole] * 3,
         out_specs=vmem,
         scratch_shapes=[
             pltpu.VMEM((devices // 8, 2 * GY, 8 * LANES), bf16),
@@ -292,59 +386,39 @@
             *[pltpu.VMEM((rows, LANES), f32)] * 8,
             pltpu.VMEM((devices, 1, LANES), f32),
             pltpu.VMEM((devices, 1, LANES), f32),
+            pltpu.VMEM((STEN, BLK, sblocks), f32),
+            pltpu.VMEM((BLK, BLK, nears), f32),
+            pltpu.VMEM((2, *panels), f32),
+            pltpu.VMEM((2 * devices, LANES), jnp.int32),
+            pltpu.VMEM((devices, LANES), jnp.int32),
+            pltpu.VMEM((devices, LANES), f32),
+            pltpu.VMEM((devices, 1, LANES), f32),
+            pltpu.VMEM((2, devices, sblocks), bf16),
+            pltpu.VMEM((STEN, sblocks), f32),
+            pltpu.VMEM((BLK, nears), f32),
             pltpu.SemaphoreType.DMA((6,)),
             pltpu.SemaphoreType.DMA((6,)),
-            pltpu.SemaphoreType.DMA,
+            pltpu.SemaphoreType.DMA((2,)),
+            pltpu.SemaphoreType.DMA((2,)),
+            pltpu.SemaphoreType.DMA((3,)),
         ],
         compiler_params=pltpu.CompilerParams(
-            collective_id=0, has_side_effects=True, vmem_limit_bytes=48 * 1024 * 1024
+            collective_id=0, has_side_effects=True, vmem_limit_bytes=60 * 1024 * 1024
         ),
-    )(outgoing, stencil_cells, jnp.asarray(lane_parts(table)), jnp.asarray(lane_parts(table.T)), green_spectrum)
-
-
-def per_device(
-    charges,
-    projection,
-    stencil_block,
-    stencil_dest,
-    stencil_cells,
-    green_spectrum,
-    near_blocks,
-    near_target,
-    near_source,
-):
-    devices = lax.axis_size(("grp", "slab"))
-    sblocks = stencil_block.shape[0]
-    capacity = stencil_cells.shape[0] // devices
-    panel_rows = charges.reshape(-1, BLK)
-    pblocks = panel_rows.shape[0]
-    owning = one_hot_rows(stencil_block, pblocks)
-    gathered = jnp.dot(owning, panel_rows, precision=highest)
-    values = jnp.sum(projection * gathered[:, None, :], axis=2)
-    target = stencil_dest[:, 0]
-    matches = one_hot_rows(target, devices)
-    triangle = (jnp.arange(sblocks)[:, None] >= jnp.arange(sblocks)[None, :]).astype(jnp.float32)
-    running = jnp.dot(triangle, matches, precision=highest)
-    ranking = (jnp.sum(running * matches, axis=1) - 1.0).astype(jnp.int32)
-    position = target * capacity + ranking
-    placing = (
-        jnp.arange(devices * capacity, dtype=jnp.int32)[:, None] == position[None, :]
-    ).astype(jnp.float32)
-    outgoing = jnp.dot(placing, values, precision=highest).reshape(devices, 1, capacity * STEN)
-    cell_rows = stencil_cells.reshape(devices, 1, capacity * STEN)
-    slab = lax.axis_size("slab")
-    returned = far_grid(outgoing, cell_rows, green_spectrum, devices, slab).reshape(devices * capacity, STEN)
-    at_stencil = lax.dot_general(placing, returned, (((0,), (0,)), ((), ())), precision=highest)
-    far_terms = jnp.sum(projection * at_stencil[:, :, None], axis=1)
-    far_field = lax.dot_general(owning, far_terms, (((0,), (0,)), ((), ())), precision=highest)
-    extended = with_halo(charges, ((("grp", "slab"), 0),), charges.shape[0]).reshape(-1, BLK)
-    sources = jnp.dot(one_hot_rows(near_source, extended.shape[0]), extended, precision=highest)
-    near_terms = jnp.sum(near_blocks * sources[:, None, :], axis=2)
-    receiver = (jnp.arange(pblocks, dtype=jnp.int32)[:, None] == near_target[None, :]).astype(
-        jnp.float32
+    )(
+        charges.reshape(panels),
+        stencil_block.reshape(1, sblocks),
+        stencil_dest.reshape(1, sblocks),
+        near_target.reshape(1, nears),
+        near_source.reshape(1, nears),
+        stencil_cells.T,
+        jnp.asarray(lane_parts(table)),
+        jnp.asarray(lane_parts(table.T)),
+        jnp.transpose(projection, (1, 2, 0)),
+        jnp.transpose(near_blocks, (1, 2, 0)),
+        green_spectrum,
     )
-    near_field = jnp.dot(receiver, near_terms, precision=highest)
-    return (far_field + near_field).reshape(-1)
+    return result.reshape(-1)
 
 
 def solution(mesh):
@@ -360,5 +434,5 @@
         P(("grp", "slab")),
     )
     return jax.shard_map(
-        per_device, mesh=mesh, in_specs=placed, out_specs=P(("grp", "slab")), check_vma=False
+        functools.partial(per_device, mesh.shape["slab"], mesh.size), mesh=mesh, in_specs=placed, out_specs=P(("grp", "slab")), check_vma=False
     )

time: 108 us -> 90.1 us (0.83)
  starting transfers between devices: 6.55 us -> 0 us
  other arithmetic: 6.45 us -> 0 us
  local copies, waits for them, and re-layouts: 4.68 us -> 1.32 us
  matrix products: 3.09 us -> 0 us
  Pallas kernels: 87 us -> 88.3 us
    ppermute x2 -> x0, starting transfers between devices: 6.55 us -> none  [the longest x1 4.63 us: with_halo(): before = lax.ppermute(last, axis, up)]
    reduce_sum x3 -> x0, other arithmetic: 4.98 us -> none  [the longest x1 2.84 us: per_device(): near_terms = jnp.sum(near_blocks * sources[:, None, :], axis=2)]
    dot_general x7 -> x0, matrix products: 3.09 us -> none  [the longest x1 0.91 us: per_device(): gathered = jnp.dot(owning, panel_rows, precision=highest)]
    reshape x5 -> x0, local copies, waits for them, and re-layouts: 1.71 us -> none  [the longest x1 0.79 us: per_device(): panel_rows = charges.reshape(-1, BLK)]
    pallas_call x1, Pallas kernels: 87 us -> 88.3 us  [per_device(): pl.pallas_call(functools.partial(whole_kernel, devices, slab), out_shape=...]
    unnamed x17 -> x1, local copies, waits for them, and re-layouts: 2.31 us -> 1.32 us
  transfers between devices with their start and end apart: 2 -> 0, of which waited for: 0 -> 0; matrix products, arithmetic and copies ran while one was open for 7% -> 0% of each run, Pallas kernels for 81% -> 0%
where the time goes in v2:
time: 90.1 us; the launch traced here: 89.6 us
  Pallas kernels  88.3 us (98%)
  local copies, waits for them, and re-layouts  1.32 us (1%)
    pallas_call x1, Pallas kernels, per_device(): pl.pallas_call(functools.partial(whole_kernel, devices, slab), out_shape=...  88.3 us

profile of v2, /device:TPU:1, one launch (start us, length us, event | category | flops | bytes accessed | tf_op | source)
XLA Modules:
  0.0 89.6 jit_solution(12869669844292885477)
XLA Ops:
  0.0 88.3 %shard_map.109 = f32[32,128]{1,0:T(8,128)} custom-call(f32[32,128]{1,0:T(8,128)} %bitcast.13, s32[1,128]{1,0:T(1,128)} %bitcast.16, s32[1,128]{1,0:T(1,128)} %bitcast.17, s32[1,256]{1,0:T(1,128)} %bitcast.14, s32[1,256]{1,0:T(1,128)} %bitcast.15, s32[64,256]{1,0:T(8,128)} %bitcast.11, f32[2,512,128]{2,1,0:T(8,128)} %constant.4.clone.table, ...), custom_call_target="tpu_custom_call" | custom-call | tf_op jit(solution)/shard_map/pallas_call | solution.py:367
  88.3 1.3 %copy.13 = f32[4096]{0:T(1024)} copy(f32[4096]{0:T(1024)} %bitcast.12) | data formatting | bytes 32768
